TPU v7x, 32 devices: a whole 2x2x4 slice. The times are simulated.
32 devices in a mesh: dp: 4 (over z), row: 2 (over core), col: 4 (over y, x).
Axes of the slice: x: 2, y: 2, z: 4, core: 2. Of those that a mesh axis runs over, the one named last changes fastest.
Arguments:
- tokens: float32 [1024, 1024], P(('dp', 'row'), 'col'), may hold values from -6 to 6
- segment_ids: int32 [1024], P('dp'), may hold values from 0 to 1023, as said below
- norm_gain: float32 [1024], P('col'), may hold values from 0.5 to 1.5
- in_weight: bfloat16 [1024, 3, 1024], P('col', None, 'row'), may hold values from -0.1875 to 0.1875
- conv_taps: float32 [3, 1024], P(None, ('row', 'col')), may hold values from -3 to 3
- out_weight: bfloat16 [1024, 1024], P('row', 'col'), may hold values from -0.1875 to 0.1875
- ffn_gain: float32 [1024], P('col'), may hold values from 0.5 to 1.5
- gate_weight: bfloat16 [1024, 4608], P('col', 'row'), may hold values from -0.1875 to 0.1875
- up_weight: bfloat16 [1024, 4608], P('col', 'row'), may hold values from -0.1875 to 0.1875
- down_weight: bfloat16 [4608, 1024], P('row', 'col'), may hold values from -0.09375 to 0.09375
- out_grad: float32 [1024, 1024], P(('dp', 'row'), 'col'), may hold values from -6 to 6
Outputs:
- block_out: float32 [1024, 1024], P(('dp', 'row'), 'col')
- in_grad: float32 [1024, 1024], P(('dp', 'row'), 'col')
- grad_norm_gain: float32 [1024], P('col')
- grad_in_weight: float32 [1024, 3, 1024], P('col', None, 'row')
- grad_conv_taps: float32 [3, 1024], P(None, ('row', 'col'))
- grad_out_weight: float32 [1024, 1024], P('row', 'col')
- grad_ffn_gain: float32 [1024], P('col')
- grad_gate_weight: float32 [1024, 4608], P('col', 'row')
- grad_up_weight: float32 [1024, 4608], P('col', 'row')
- grad_down_weight: float32 [4608, 1024], P('row', 'col')
Inputs may be any that keep to these rules, and one draw needn't show every extreme that they name: `segment_ids`: ids never fall along the tokens; every aligned sequence of 256 consecutive tokens starts a new id and changes id again at least once inside; runs of one id have 200 to 2000 tokens except where a sequence's start or end cuts them; the last token's id is 1023.
All inputs are finite; a program needn't handle non-finite values.
Results may differ from a plain program's by a relative error of at most 0.0094.
Values may be sent and summed in bfloat16 or wider, within the bound.
No kernel may reach another device: no remote copies, remote signals or barrier semaphores. Data moves between devices by JAX's collectives and lax.ppermute only.
A program may use at most 128 MiB of HBM per device.

v0:
```python
import jax
import jax.numpy as jnp
from jax import lax
from jax.sharding import PartitionSpec as P

D = 1024
epsilon = 1e-05


def shifted(source, amount):
    filler = jnp.zeros((amount,) + source.shape[1:], source.dtype)
    return jnp.concatenate([filler, source[:-amount]], axis=0)


def lifted(source, amount):
    filler = jnp.zeros((amount,) + source.shape[1:], source.dtype)
    return jnp.concatenate([source[amount:], filler], axis=0)


def dot_rows(left, right):
    return lax.dot_general(
        left, right, (((0,), (0,)), ((), ())), preferred_element_type=jnp.float32
    )


def dot_cols(left, right):
    return lax.dot_general(
        left, right, (((1,), (1,)), ((), ())), preferred_element_type=jnp.float32
    )


def sum_rows(entries):
    return lax.psum(jnp.sum(entries, axis=1, keepdims=True), "col")


def gather_rows(shard_part):
    return lax.all_gather(shard_part, "row", axis=0, tiled=True)


def reduce_cols(partial_value):
    return lax.psum_scatter(partial_value, "col", scatter_dimension=2, tiled=True)


def share_cols(shard_part):
    return lax.all_gather(shard_part, "col", axis=2, tiled=True)


def reduce_rows(term, local_rows):
    return lax.psum_scatter(
        term(jnp.int32(0), lax.axis_size("row") * local_rows),
        "row",
        scatter_dimension=0,
        tiled=True,
    )


def per_device(
    tokens,
    segment_ids,
    norm_gain,
    in_weight,
    conv_taps,
    out_weight,
    ffn_gain,
    gate_weight,
    up_weight,
    down_weight,
    out_grad,
):
    local_rows = tokens.shape[0]
    same_one = jnp.concatenate(
        [jnp.zeros((1,), jnp.float32), (segment_ids[1:] == segment_ids[:-1]).astype(jnp.float32)]
    )[:, None]
    same_two = jnp.concatenate(
        [jnp.zeros((2,), jnp.float32), (segment_ids[2:] == segment_ids[:-2]).astype(jnp.float32)]
    )[:, None]
    in_flat = in_weight.reshape(in_weight.shape[0], -1)
    scale_one = lax.rsqrt(sum_rows(tokens * tokens) / D + epsilon)
    normed_one = (tokens * scale_one * norm_gain).astype(jnp.bfloat16)
    normed_one_all = gather_rows(normed_one)
    group_rows = normed_one_all.shape[0]
    mixer_in = reduce_cols(
        jnp.dot(normed_one_all, in_flat, preferred_element_type=jnp.float32).reshape(
            group_rows, 3, -1
        )
    )
    gate_in = mixer_in[:, 0]
    gate_out = mixer_in[:, 1]
    carried = mixer_in[:, 2]
    product = gate_in * carried
    conv_out = (
        conv_taps[2] * product
        + conv_taps[1] * shifted(product, 1) * same_one
        + conv_taps[0] * shifted(product, 2) * same_two
    )
    mixed = (gate_out * conv_out).astype(jnp.bfloat16)
    mixed_all = share_cols(mixed[:, None, :])[:, 0, :]

    def mixer_fwd(offset, length):
        return jnp.dot(mixed_all, out_weight, preferred_element_type=jnp.float32)

    hidden_mid = tokens + reduce_rows(mixer_fwd, local_rows)
    scale_two = lax.rsqrt(sum_rows(hidden_mid * hidden_mid) / D + epsilon)
    normed_two = (hidden_mid * scale_two * ffn_gain).astype(jnp.bfloat16)
    normed_two_all = gather_rows(normed_two)
    both_proj = reduce_cols(
        jnp.stack(
            [
                jnp.dot(normed_two_all, gate_weight, preferred_element_type=jnp.float32),
                jnp.dot(normed_two_all, up_weight, preferred_element_type=jnp.float32),
            ],
            axis=1,
        )
    )
    gate_proj = both_proj[:, 0]
    up_proj = both_proj[:, 1]
    sigmoid_gate = jax.nn.sigmoid(gate_proj)
    activated = (gate_proj * sigmoid_gate * up_proj).astype(jnp.bfloat16)
    activated_all = share_cols(activated[:, None, :])[:, 0, :]

    def ffn_fwd(offset, length):
        return jnp.dot(activated_all, down_weight, preferred_element_type=jnp.float32)

    block_out = hidden_mid + reduce_rows(ffn_fwd, local_rows)
    grad_ffn = out_grad.astype(jnp.bfloat16)
    grad_ffn_all = gather_rows(grad_ffn)
    grad_down = dot_rows(activated_all, grad_ffn_all)
    grad_act = reduce_cols(dot_cols(grad_ffn_all, down_weight)[:, None, :])[:, 0, :]
    grad_up = grad_act * gate_proj * sigmoid_gate
    grad_gate = grad_act * up_proj * sigmoid_gate * (1.0 + gate_proj * (1.0 - sigmoid_gate))
    grad_pair = jnp.stack([grad_gate, grad_up], axis=1).astype(jnp.bfloat16)
    grad_pair_all = share_cols(grad_pair)
    grad_gate_w = dot_rows(normed_two_all, grad_pair_all[:, 0])
    grad_up_w = dot_rows(normed_two_all, grad_pair_all[:, 1])

    def ffn_back(offset, length):
        return dot_cols(grad_pair_all[:, 0], gate_weight) + dot_cols(grad_pair_all[:, 1], up_weight)

    grad_normed_two = reduce_rows(ffn_back, local_rows)
    gain_two_grad = jnp.sum(grad_normed_two * hidden_mid * scale_two, axis=0)
    weighted_two = ffn_gain * grad_normed_two
    cube_two = scale_two * scale_two * scale_two
    grad_mid = (
        out_grad
        + scale_two * weighted_two
        - hidden_mid * cube_two * (sum_rows(weighted_two * hidden_mid) / D)
    )
    grad_mix = grad_mid.astype(jnp.bfloat16)
    grad_mix_all = gather_rows(grad_mix)
    grad_out_w = dot_rows(mixed_all, grad_mix_all)
    grad_mixed = reduce_cols(dot_cols(grad_mix_all, out_weight)[:, None, :])[:, 0, :]
    grad_conv = grad_mixed * gate_out
    grad_product = (
        conv_taps[2] * grad_conv
        + conv_taps[1] * lifted(grad_conv * same_one, 1)
        + conv_taps[0] * lifted(grad_conv * same_two, 2)
    )
    taps_grad = jnp.stack(
        [
            jnp.sum(grad_conv * shifted(product, 2) * same_two, axis=0),
            jnp.sum(grad_conv * shifted(product, 1) * same_one, axis=0),
            jnp.sum(grad_conv * product, axis=0),
        ]
    )
    grad_triple = jnp.stack(
        [grad_product * carried, grad_mixed * conv_out, grad_product * gate_in], axis=1
    ).astype(jnp.bfloat16)
    grad_triple_all = share_cols(grad_triple)
    flat_grad = grad_triple_all.reshape(group_rows, -1)
    grad_in_w = dot_rows(normed_one_all, flat_grad).reshape(in_weight.shape)

    def mixer_back(offset, length):
        return dot_cols(flat_grad, in_flat)

    grad_normed_one = reduce_rows(mixer_back, local_rows)
    gain_one_grad = jnp.sum(grad_normed_one * tokens * scale_one, axis=0)
    weighted_one = norm_gain * grad_normed_one
    cube_one = scale_one * scale_one * scale_one
    in_grad = (
        grad_mid
        + scale_one * weighted_one
        - tokens * cube_one * (sum_rows(weighted_one * tokens) / D)
    )
    summed = lax.psum((grad_in_w, taps_grad, grad_out_w, grad_gate_w, grad_up_w, grad_down), "dp")
    gain_sums = lax.psum((gain_one_grad, gain_two_grad), ("dp", "row"))
    return (
        block_out,
        in_grad,
        gain_sums[0],
        summed[0],
        summed[1],
        summed[2],
        gain_sums[1],
        summed[3],
        summed[4],
        summed[5],
    )


def solution(mesh):
    in_specs = (
        P(("dp", "row"), "col"),
        P("dp"),
        P("col"),
        P("col", None, "row"),
        P(None, ("row", "col")),
        P("row", "col"),
        P("col"),
        P("col", "row"),
        P("col", "row"),
        P("row", "col"),
        P(("dp", "row"), "col"),
    )
    out_specs = (
        P(("dp", "row"), "col"),
        P(("dp", "row"), "col"),
        P("col"),
        P("col", None, "row"),
        P(None, ("row", "col")),
        P("row", "col"),
        P("col"),
        P("col", "row"),
        P("col", "row"),
        P("row", "col"),
    )
    return jax.shard_map(
        per_device, mesh=mesh, in_specs=in_specs, out_specs=out_specs, check_vma=False
    )
```

profile of v0, /device:TPU:0, one launch (start us, length us, event | category | flops | bytes accessed | tf_op | source)
XLA Modules:
  0.0 744.6 jit_solution(4233200987819264704)
XLA Ops:
  8.9 11.4 %psum.84 = f32[128,1]{0,1:T(1,128)S(1)} all-reduce(f32[128,1]{0,1:T(1,128)S(1)} %bitcast.150), channel_id=1, replica_groups=mesh['dp'=4,'row'=2,'col'=4] {'col'}, use_global_device_ids=true, to_apply=%region_1.0 | all-reduce | flops 128 | bytes 1024 | tf_op jit(solution)/shard_map/psum | solution.py:33
  25.8 30.3 %reduce-scatter.7.cloned.1.call-done = f32[256,3,128]{2,0,1:T(8,128)} async-done(((f32[256,3,512]{2,0,1:T(8,128)}), f32[256,3,128]{2,0,1:T(8,128)}) %reduce-scatter.7.cloned.1.call-update) | async-done | bytes 393232 | tf_op jit(solution)/shard_map/reduce_scatter | solution.py:41
  59.6 9.0 %all-gather = bf16[256,512]{1,0:T(8,128)(2,1)S(1)} all-gather(bf16[256,128]{1,0:T(8,128)(2,1)S(1)} %get-tuple-element.33), channel_id=2, replica_groups=mesh['dp'=4,'row'=2,'col'=4] {'col'}, dimensions={1}, use_global_device_ids=true | all-gather | bytes 327680 | tf_op jit(solution)/shard_map/all_gather | solution.py:45
  74.8 3.9 copy.43
  79.8 9.5 %psum.85 = f32[128,1]{0,1:T(1,128)S(1)} all-reduce(f32[128,1]{0,1:T(1,128)S(1)} %bitcast.147), channel_id=1, replica_groups=mesh['dp'=4,'row'=2,'col'=4] {'col'}, use_global_device_ids=true, to_apply=%region_5.0 | all-reduce | flops 128 | bytes 1024 | tf_op jit(solution)/shard_map/psum | solution.py:33
  93.6 2.5 pad_maximum_fusion
  96.1 8.1 %copy.40 = f32[256,2,2304]{0,1,2:T(2,128)} copy(f32[256,2,2304]{2,0,1:T(8,128)} %pad_maximum_fusion) | data formatting | bytes 9437184 | tf_op jit(solution)/shard_map/stack | solution.py:107
  106.1 148.5 %all-reduce.13.cloned.1.call-done = (f32[256,2,2304]{0,1,2:T(2,128)}, f32[256,1,2304]{0,1,2:T(1,128)}) async-done(((f32[256,2,2304]{0,1,2:T(2,128)}, f32[256,1,2304]{0,1,2:T(1,128)}), (f32[256,2,2304]{0,1,2:T(2,128)}, f32[256,1,2304]{0,1,2:T(1,128)})) %all-reduce.13.cloned.1.call-update) | async-done | bytes 7077904
  256.1 2.7 constant_dynamic-slice_fusion
  262.0 37.0 %all-gather.6.cloned.1.call-done = bf16[256,2,2304]{0,1,2:T(2,128)(2,1)} async-done(((bf16[256,2,576]{0,1,2:T(2,128)(2,1)}), bf16[256,2,2304]{0,1,2:T(2,128)(2,1)}) %all-gather.6.cloned.1.call-update) | async-done | bytes 2359312 | tf_op jit(solution)/shard_map/all_gather | solution.py:45
  299.0 7.9 %fusion.31 = (bf16[256,1,2304]{0,1,2:T(2,128)(2,1)}, bf16[256,1,2304]{0,1,2:T(2,128)(2,1)}) fusion(bf16[256,2,2304]{0,1,2:T(2,128)(2,1)} %all-gather.6.cloned.1.call-done), kind=kLoop, calls=%fused_computation.83 | loop fusion | bytes 4718592 | tf_op jit(solution)/shard_map/slice | solution.py:137
  306.9 5.0 copy.56
  311.9 5.0 copy.55
  319.4 9.4 %all-gather.4.cloned.1.call-done = bf16[256,1,2304]{0,2,1:T(8,128)(2,1)} async-done(((bf16[256,1,576]{0,2,1:T(8,128)(2,1)}), bf16[256,1,2304]{0,2,1:T(8,128)(2,1)}) %all-gather.4.cloned.1.call-update) | async-done | bytes 1179664 | tf_op jit(solution)/shard_map/all_gather | solution.py:45
  331.4 7.9 %reduce-scatter.13.cloned.1.call-done = f32[128,256]{1,0:T(8,128)} async-done(((f32[256,256]{1,0:T(8,128)}), f32[128,256]{1,0:T(8,128)}) %reduce-scatter.13.cloned.1.call-update) | async-done | bytes 131088 | tf_op jit(solution)/shard_map/reduce_scatter | solution.py:49
  341.0 10.6 %psum.86 = f32[128,1]{0,1:T(1,128)} all-reduce(f32[128,1]{0,1:T(1,128)} %bitcast.148), channel_id=1, replica_groups=mesh['dp'=4,'row'=2,'col'=4] {'col'}, use_global_device_ids=true, to_apply=%region_11.0 | all-reduce | flops 128 | bytes 1024 | tf_op jit(solution)/shard_map/psum | solution.py:33
  360.6 2.8 fusion.8
  367.3 16.6 %reduce-scatter.15.cloned.1.call-done = f32[256,1,128]{2,0,1:T(8,128)} async-done(((f32[256,1,512]{2,0,1:T(8,128)}), f32[256,1,128]{2,0,1:T(8,128)}) %reduce-scatter.15.cloned.1.call-update) | async-done | bytes 131088 | tf_op jit(solution)/shard_map/reduce_scatter | solution.py:41
  385.3 11.5 %all_gather.31 = bf16[256,3,512]{2,0,1:T(8,128)(2,1)S(1)} all-gather(bf16[256,3,128]{2,0,1:T(8,128)(2,1)S(1)} %pad_maximum_fusion.2), channel_id=1, replica_groups=mesh['dp'=4,'row'=2,'col'=4] {'col'}, dimensions={2}, use_global_device_ids=true | all-gather | bytes 983040 | tf_op jit(solution)/shard_map/all_gather | solution.py:45
  401.0 12.4 %psum.90 = f32[3,128]{1,0:T(4,128)} all-reduce(f32[3,128]{1,0:T(4,128)S(1)} %pad_maximum_fusion.3), channel_id=1, replica_groups=mesh['dp'=4,'row'=2,'col'=4] {'dp'}, use_global_device_ids=true, to_apply=%region_22.0 | all-reduce | flops 384 | bytes 3072 | tf_op jit(solution)/shard_map/psum | solution.py:184
  414.4 8.9 %psum.87 = f32[128,1]{0,1:T(1,128)S(1)} all-reduce(f32[128,1]{0,1:T(1,128)S(1)} %bitcast.149), channel_id=1, replica_groups=mesh['dp'=4,'row'=2,'col'=4] {'col'}, use_global_device_ids=true, to_apply=%region_15.0 | all-reduce | flops 128 | bytes 1024 | tf_op jit(solution)/shard_map/psum | solution.py:33
  423.4 14.9 %all-reduce.7 = (f32[256]{0:T(256)}, f32[256]{0:T(256)}) all-reduce(f32[256]{0:T(256)S(1)} %get-tuple-element.12, f32[256]{0:T(256)S(1)} %copy-done.42), channel_id=1, replica_groups=mesh['dp'=4,'row'=2,'col'=4] {'dp','row'}, use_global_device_ids=true, to_apply=%region_17.0 | all-reduce | flops 512 | bytes 4096 | tf_op jit(solution)/shard_map/psum | solution.py:185
  440.0 287.7 %all-reduce.15.cloned.1.call-done = (f32[256,3,512]{2,0,1:T(8,128)}, f32[512,256]{1,0:T(8,128)}, f32[256,2304]{1,0:T(8,128)}, f32[256,2304]{1,0:T(8,128)}, f32[2304,256]{1,0:T(8,128)}) async-done(((f32[256,3,512]{2,0,1:T(8,128)}, f32[512,256]{1,0:T(8,128)}, f32[256,2304]{1,0:T(8,128)}, f32[256,2304]{1,0:T(8,128)}, f32[2304,256]{1,0:T(8,128)}), (f32[256,3,512]{2,0,1:T(8,128)}, f32[512,256]{1,0:T(8,128)}, ...) | async-done | bytes 9175056 | tf_op jit(solution)/shard_map/psum | solution.py:184
  727.7 2.8 copy.71
  (176 shorter events, 62.9 us)
Async XLA Ops:
  7.2 84.7 %copy-start = (bf16[256,2304]{1,0:T(8,128)(2,1)S(1)}, bf16[256,2304]{1,0:T(8,128)(2,1)}, u32[]{:S(2)}) copy-start(bf16[256,2304]{1,0:T(8,128)(2,1)} %param.19) | copy-start | bytes 3538948
  7.2 48.9 %reduce-scatter.7.cloned.1.call-start = ((), (), s32[]{:S(2)}) async-start(), calls=%async_computation.6 | async-start | bytes 1966080 | tf_op jit(solution)/shard_map/reduce_scatter | solution.py:41
  25.5 43.9 %copy-start.25 = (bf16[512,256]{1,0:T(8,128)(2,1)S(1)}, bf16[512,256]{1,0:T(8,128)(2,1)}, u32[]{:S(2)}) copy-start(bf16[512,256]{1,0:T(8,128)(2,1)} %param.16) | copy-start | bytes 786436
  25.5 44.9 %copy-start.29 = (f32[128,256]{1,0:T(8,128)S(1)}, f32[128,256]{1,0:T(8,128)}, u32[]{:S(2)}) copy-start(f32[128,256]{1,0:T(8,128)} %param.21) | copy-start | bytes 393220
  25.5 53.2 %reduce-scatter.9.cloned.1.call-start = ((), (), s32[]{:S(2)}) async-start(), calls=%async_computation.7 | async-start | bytes 393216 | tf_op jit(solution)/shard_map/reduce_scatter | solution.py:49
  25.8 44.6 %copy-start.38 = (f32[128]{0:T(128)}, f32[128]{0:T(128)S(1)}, u32[]{:S(2)}) copy-start(f32[128]{0:T(128)S(1)} %get-tuple-element.45) | copy-start | bytes 1540
  25.8 44.6 %copy-start.40 = (f32[128]{0:T(128)}, f32[128]{0:T(128)S(1)}, u32[]{:S(2)}) copy-start(f32[128]{0:T(128)S(1)} %get-tuple-element.46) | copy-start | bytes 1540
  25.8 46.5 %copy-start.36 = (f32[128]{0:T(128)}, f32[128]{0:T(128)S(1)}, u32[]{:S(2)}) copy-start(f32[128]{0:T(128)S(1)} %get-tuple-element.44) | copy-start | bytes 1540
  70.3 184.3 %all-reduce.13.cloned.1.call-start = ((), (), s32[]{:S(2)}) async-start(), calls=%async_computation.14 | async-start | bytes 14155776
  104.3 194.7 %all-gather.6.cloned.1.call-start = ((), (), s32[]{:S(2)}) async-start(), calls=%async_computation.10 | async-start | bytes 2949120 | tf_op jit(solution)/shard_map/all_gather | solution.py:45
  261.4 67.5 %all-gather.4.cloned.1.call-start = ((), (), s32[]{:S(2)}) async-start(), calls=%async_computation.8 | async-start | bytes 1474560 | tf_op jit(solution)/shard_map/all_gather | solution.py:45
  261.9 77.3 %reduce-scatter.13.cloned.1.call-start = ((), (), s32[]{:S(2)}) async-start(), calls=%async_computation.11 | async-start | bytes 393216 | tf_op jit(solution)/shard_map/reduce_scatter | solution.py:49
  319.4 33.4 %reduce-scatter.11.cloned.1.call-start = ((), (), s32[]{:S(2)}) async-start(), calls=%async_computation.9 | async-start | bytes 393216 | tf_op jit(solution)/shard_map/reduce_scatter | solution.py:49
  331.4 29.2 %copy-start.5 = (bf16[256,1,2304]{0,2,1:T(8,128)(2,1)S(1)}, bf16[256,1,2304]{0,2,1:T(8,128)(2,1)}, u32[]{:S(2)}) copy-start(bf16[256,1,2304]{0,2,1:T(8,128)(2,1)} %all-gather.4.cloned.1.call-done) | copy-start | bytes 3538948
  331.4 52.5 %reduce-scatter.15.cloned.1.call-start = ((), (), s32[]{:S(2)}) async-start(), calls=%async_computation.12 | async-start | bytes 655360 | tf_op jit(solution)/shard_map/reduce_scatter | solution.py:41
  359.3 54.1 %reduce-scatter.17.cloned.1.call-start = ((), (), s32[]{:S(2)}) async-start(), calls=%async_computation.13 | async-start | bytes 393216 | tf_op jit(solution)/shard_map/reduce_scatter | solution.py:49
  365.3 18.6 %copy-start.12 = (f32[256,128]{1,0:T(8,128)S(1)}, f32[256,128]{1,0:T(8,128)}, u32[]{:S(2)}) copy-start(f32[256,128]{1,0:T(8,128)} %copy-done.11) | copy-start | bytes 393220
  365.3 18.6 %copy-start.27 = (f32[256,128]{1,0:T(8,128)S(1)}, f32[256,128]{1,0:T(8,128)}, u32[]{:S(2)}) copy-start(f32[256,128]{1,0:T(8,128)} %get-tuple-element.34) | copy-start | bytes 393220
  365.3 19.6 %copy-start.44 = (f32[254]{0:T(256)S(1)}, f32[254]{0:T(256)}, u32[]{:S(2)}) copy-start(f32[254]{0:T(256)} %slice.89) | copy-start | bytes 3052
  365.3 19.7 %copy-start.43 = (f32[255]{0:T(256)S(1)}, f32[255]{0:T(256)}, u32[]{:S(2)}) copy-start(f32[255]{0:T(256)} %slice.87) | copy-start | bytes 3064
  397.9 329.8 %all-reduce.15.cloned.1.call-start = ((), (), s32[]{:S(2)}) async-start(), calls=%async_computation.15 | async-start | bytes 18350080 | tf_op jit(solution)/shard_map/psum | solution.py:184
  400.9 22.4 %copy-start.42 = (f32[256]{0:T(256)S(1)}, f32[256]{0:T(256)}, u32[]{:S(2)}) copy-start(f32[256]{0:T(256)} %get-tuple-element.10) | copy-start | bytes 3076
  400.9 37.4 %copy-start.28 = (f32[128,256]{1,0:T(8,128)S(1)}, f32[128,256]{1,0:T(8,128)}, u32[]{:S(2)}) copy-start(f32[128,256]{1,0:T(8,128)} %get-tuple-element.30) | copy-start | bytes 393220
  400.9 37.4 %copy-start.46 = (f32[128]{0:T(128)S(1)}, f32[128]{0:T(128)}, u32[]{:S(2)}) copy-start(f32[128]{0:T(128)} %get-tuple-element.47) | copy-start | bytes 1540
  (34 other events, 221.5 us)
Sparse Core Ops, SparseCore 0:
  25.6 30.4 reduce-scatter.6
  70.4 7.7 reduce-scatter.8
  104.4 150.2 all-reduce.12
  261.5 37.4 all-gather.5
  301.3 27.5 all-gather.3
  331.5 7.7 reduce-scatter.12
  342.1 8.8 reduce-scatter.10
  359.4 24.4 reduce-scatter.14
  398.1 7.7 reduce-scatter.16
  409.9 317.7 all-reduce.14
where the time goes:
time: 746 us; the launch traced here: 745 us
  waiting for transfers between devices  538 us (72%)
  blocking collectives  95.9 us (13%)
  local copies, waits for them, and re-layouts  55.2 us (7%)
  matrix products  21.8 us (3%)
  other arithmetic  17.9 us (2%)
  between operations  15.3 us (2%)
    psum x1, waiting for transfers between devices, per_device(): lax.psum((grad_in_w, taps_grad, grad_out_w, grad_gate_w, grad_up_w, grad_...  288 us
    unnamed x11, waiting for transfers between devices  149 us
    reduce_scatter x2, waiting for transfers between devices, reduce_cols(): lax.psum_scatter(partial_value, 'col', scatter_dimension=2, tiled=True)  46.9 us
    all_gather x2, waiting for transfers between devices, share_cols(): return lax.all_gather(shard_part, 'col', axis=2, tiled=True)  46.4 us
    psum x4, blocking collectives, sum_rows(): return lax.psum(jnp.sum(entries, axis=1, keepdims=True), 'col')  40.5 us
    unnamed x106, local copies, waits for them, and re-layouts  29.6 us
    all_gather x2, blocking collectives, share_cols(): return lax.all_gather(shard_part, 'col', axis=2, tiled=True)  20.5 us
    psum x1, blocking collectives, per_device(): gain_sums = lax.psum((gain_one_grad, gain_two_grad), ('dp', 'row'))  14.9 us
  transfers between devices with their start and end apart: 10, of which 7 were waited for; matrix products, arithmetic and copies ran while one was open for 6% of the time, Pallas kernels for 0%

commit v1 on v0

--- a/solution.py
+++ b/solution.py
@@ -30,7 +30,7 @@
 
 
 def sum_rows(entries):
-    return lax.psum(jnp.sum(entries, axis=1, keepdims=True), "col")
+    return jnp.sum(lax.all_gather(jnp.sum(entries, axis=1, keepdims=True), "col"), 0)
 
 
 def gather_rows(shard_part):

time: 746 us -> 744 us (level)
  blocking collectives: 95.9 us -> 87.7 us
    psum x4 -> x0, blocking collectives: 40.5 us -> none  [sum_rows(): return lax.psum(jnp.sum(entries, axis=1, keepdims=True), 'col')]
    all_gather x0 -> x4, blocking collectives: none -> 32.2 us  [sum_rows(): lax.all_gather(jnp.sum(entries, axis=1, keepdims=True), 'col')]
where the time goes in v1:
time: 744 us; the launch traced here: 742 us
  waiting for transfers between devices  543 us (73%)
  blocking collectives  87.7 us (12%)
  local copies, waits for them, and re-layouts  55.2 us (7%)
  matrix products  21.8 us (3%)
  other arithmetic  19.2 us (3%)
  between operations  15.3 us (2%)
    psum x1, waiting for transfers between devices, per_device(): lax.psum((grad_in_w, taps_grad, grad_out_w, grad_gate_w, grad_up_w, grad_...  290 us
    unnamed x11, waiting for transfers between devices  150 us
    reduce_scatter x2, waiting for transfers between devices, reduce_cols(): lax.psum_scatter(partial_value, 'col', scatter_dimension=2, tiled=True)  48.9 us
    all_gather x2, waiting for transfers between devices, share_cols(): return lax.all_gather(shard_part, 'col', axis=2, tiled=True)  46.4 us
    all_gather x4, blocking collectives, sum_rows(): lax.all_gather(jnp.sum(entries, axis=1, keepdims=True), 'col')  32.2 us
    unnamed x106, local copies, waits for them, and re-layouts  29.6 us
    all_gather x2, blocking collectives, share_cols(): return lax.all_gather(shard_part, 'col', axis=2, tiled=True)  20.5 us
    psum x1, blocking collectives, per_device(): gain_sums = lax.psum((gain_one_grad, gain_two_grad), ('dp', 'row'))  15.1 us
  transfers between devices with their start and end apart: 10, of which 7 were waited for; matrix products, arithmetic and copies ran while one was open for 6% of the time, Pallas kernels for 0%

profile of v1, /device:TPU:0, one launch (start us, length us, event | category | flops | bytes accessed | tf_op | source)
XLA Modules:
  0.0 742.5 jit_solution(18262495066495899412)
XLA Ops:
  8.9 9.4 %all-gather.5 = f32[4,1,128]{2,1,0:T(1,128)S(1)} all-gather(f32[1,1,128]{2,1,0:T(1,128)S(1)} %bitcast.138), channel_id=2, replica_groups=mesh['dp'=4,'row'=2,'col'=4] {'col'}, dimensions={0}, use_global_device_ids=true | all-gather | bytes 2560 | tf_op jit(solution)/shard_map/all_gather | solution.py:33
  23.9 31.3 %reduce-scatter.7.cloned.1.call-done = f32[256,3,128]{2,0,1:T(8,128)} async-done(((f32[256,3,512]{2,0,1:T(8,128)}), f32[256,3,128]{2,0,1:T(8,128)}) %reduce-scatter.7.cloned.1.call-update) | async-done | bytes 393232 | tf_op jit(solution)/shard_map/reduce_scatter | solution.py:41
  58.6 9.0 %all-gather.1 = bf16[256,512]{1,0:T(8,128)(2,1)S(1)} all-gather(bf16[256,128]{1,0:T(8,128)(2,1)S(1)} %get-tuple-element.33), channel_id=3, replica_groups=mesh['dp'=4,'row'=2,'col'=4] {'col'}, dimensions={1}, use_global_device_ids=true | all-gather | bytes 327680 | tf_op jit(solution)/shard_map/all_gather | solution.py:45
  73.8 3.9 copy.43
  78.8 7.6 %all-gather.6 = f32[4,1,128]{2,1,0:T(1,128)S(1)} all-gather(f32[1,1,128]{2,1,0:T(1,128)S(1)} %bitcast.135), channel_id=4, replica_groups=mesh['dp'=4,'row'=2,'col'=4] {'col'}, dimensions={0}, use_global_device_ids=true | all-gather | bytes 2560 | tf_op jit(solution)/shard_map/all_gather | solution.py:33
  90.7 2.5 pad_maximum_fusion
  93.2 8.1 %copy.40 = f32[256,2,2304]{0,1,2:T(2,128)} copy(f32[256,2,2304]{2,0,1:T(8,128)} %pad_maximum_fusion) | data formatting | bytes 9437184 | tf_op jit(solution)/shard_map/stack | solution.py:107
  103.2 149.4 %all-reduce.13.cloned.1.call-done = (f32[256,2,2304]{0,1,2:T(2,128)}, f32[256,1,2304]{0,1,2:T(1,128)}) async-done(((f32[256,2,2304]{0,1,2:T(2,128)}, f32[256,1,2304]{0,1,2:T(1,128)}), (f32[256,2,2304]{0,1,2:T(2,128)}, f32[256,1,2304]{0,1,2:T(1,128)})) %all-reduce.13.cloned.1.call-update) | async-done | bytes 7077904
  254.1 2.7 constant_dynamic-slice_fusion
  260.0 37.0 %all-gather.14.cloned.1.call-done = bf16[256,2,2304]{0,1,2:T(2,128)(2,1)} async-done(((bf16[256,2,576]{0,1,2:T(2,128)(2,1)}), bf16[256,2,2304]{0,1,2:T(2,128)(2,1)}) %all-gather.14.cloned.1.call-update) | async-done | bytes 2359312 | tf_op jit(solution)/shard_map/all_gather | solution.py:45
  297.0 7.9 %fusion.27 = (bf16[256,1,2304]{0,1,2:T(2,128)(2,1)}, bf16[256,1,2304]{0,1,2:T(2,128)(2,1)}) fusion(bf16[256,2,2304]{0,1,2:T(2,128)(2,1)} %all-gather.14.cloned.1.call-done), kind=kLoop, calls=%fused_computation.79 | loop fusion | bytes 4718592 | tf_op jit(solution)/shard_map/slice | solution.py:137
  304.9 5.0 copy.56
  309.9 5.0 copy.55
  317.4 9.4 %all-gather.12.cloned.1.call-done = bf16[256,1,2304]{0,2,1:T(8,128)(2,1)} async-done(((bf16[256,1,576]{0,2,1:T(8,128)(2,1)}), bf16[256,1,2304]{0,2,1:T(8,128)(2,1)}) %all-gather.12.cloned.1.call-update) | async-done | bytes 1179664 | tf_op jit(solution)/shard_map/all_gather | solution.py:45
  329.4 7.9 %reduce-scatter.13.cloned.1.call-done = f32[128,256]{1,0:T(8,128)} async-done(((f32[256,256]{1,0:T(8,128)}), f32[128,256]{1,0:T(8,128)}) %reduce-scatter.13.cloned.1.call-update) | async-done | bytes 131088 | tf_op jit(solution)/shard_map/reduce_scatter | solution.py:49
  338.9 8.4 %all-gather.7 = f32[4,1,128]{2,1,0:T(1,128)} all-gather(f32[1,1,128]{2,1,0:T(1,128)S(1)} %bitcast.136), channel_id=5, replica_groups=mesh['dp'=4,'row'=2,'col'=4] {'col'}, dimensions={0}, use_global_device_ids=true | all-gather | bytes 2560 | tf_op jit(solution)/shard_map/all_gather | solution.py:33
  357.5 2.8 fusion.8
  364.2 17.6 %reduce-scatter.15.cloned.1.call-done = f32[256,1,128]{2,0,1:T(8,128)} async-done(((f32[256,1,512]{2,0,1:T(8,128)}), f32[256,1,128]{2,0,1:T(8,128)}) %reduce-scatter.15.cloned.1.call-update) | async-done | bytes 131088 | tf_op jit(solution)/shard_map/reduce_scatter | solution.py:41
  383.3 11.5 %all_gather.46 = bf16[256,3,512]{2,0,1:T(8,128)(2,1)S(1)} all-gather(bf16[256,3,128]{2,0,1:T(8,128)(2,1)S(1)} %pad_maximum_fusion.2), channel_id=1, replica_groups=mesh['dp'=4,'row'=2,'col'=4] {'col'}, dimensions={2}, use_global_device_ids=true | all-gather | bytes 983040 | tf_op jit(solution)/shard_map/all_gather | solution.py:45
  398.9 12.4 %psum.58 = f32[3,128]{1,0:T(4,128)} all-reduce(f32[3,128]{1,0:T(4,128)S(1)} %pad_maximum_fusion.3), channel_id=1, replica_groups=mesh['dp'=4,'row'=2,'col'=4] {'dp'}, use_global_device_ids=true, to_apply=%region_22.0 | all-reduce | flops 384 | bytes 3072 | tf_op jit(solution)/shard_map/psum | solution.py:184
  412.4 6.7 all-gather.8
  419.1 15.1 %all-reduce.7 = (f32[256]{0:T(256)}, f32[256]{0:T(256)}) all-reduce(f32[256]{0:T(256)S(1)} %get-tuple-element.12, f32[256]{0:T(256)S(1)} %copy-done.42), channel_id=1, replica_groups=mesh['dp'=4,'row'=2,'col'=4] {'dp','row'}, use_global_device_ids=true, to_apply=%region_17.0 | all-reduce | flops 512 | bytes 4096 | tf_op jit(solution)/shard_map/psum | solution.py:185
  435.9 289.7 %all-reduce.15.cloned.1.call-done = (f32[256,3,512]{2,0,1:T(8,128)}, f32[512,256]{1,0:T(8,128)}, f32[256,2304]{1,0:T(8,128)}, f32[256,2304]{1,0:T(8,128)}, f32[2304,256]{1,0:T(8,128)}) async-done(((f32[256,3,512]{2,0,1:T(8,128)}, f32[512,256]{1,0:T(8,128)}, f32[256,2304]{1,0:T(8,128)}, f32[256,2304]{1,0:T(8,128)}, f32[2304,256]{1,0:T(8,128)}), (f32[256,3,512]{2,0,1:T(8,128)}, f32[512,256]{1,0:T(8,128)}, ...) | async-done | bytes 9175056 | tf_op jit(solution)/shard_map/psum | solution.py:184
  725.6 2.8 copy.71
  (180 shorter events, 64.2 us)
Async XLA Ops:
  7.2 81.8 %copy-start = (bf16[256,2304]{1,0:T(8,128)(2,1)S(1)}, bf16[256,2304]{1,0:T(8,128)(2,1)}, u32[]{:S(2)}) copy-start(bf16[256,2304]{1,0:T(8,128)(2,1)} %param.19) | copy-start | bytes 3538948
  7.2 47.9 %reduce-scatter.7.cloned.1.call-start = ((), (), s32[]{:S(2)}) async-start(), calls=%async_computation.6 | async-start | bytes 1966080 | tf_op jit(solution)/shard_map/reduce_scatter | solution.py:41
  23.5 44.8 %copy-start.25 = (bf16[512,256]{1,0:T(8,128)(2,1)S(1)}, bf16[512,256]{1,0:T(8,128)(2,1)}, u32[]{:S(2)}) copy-start(bf16[512,256]{1,0:T(8,128)(2,1)} %param.16) | copy-start | bytes 786436
  23.6 45.8 %copy-start.29 = (f32[128,256]{1,0:T(8,128)S(1)}, f32[128,256]{1,0:T(8,128)}, u32[]{:S(2)}) copy-start(f32[128,256]{1,0:T(8,128)} %param.21) | copy-start | bytes 393220
  23.6 54.1 %reduce-scatter.9.cloned.1.call-start = ((), (), s32[]{:S(2)}) async-start(), calls=%async_computation.7 | async-start | bytes 393216 | tf_op jit(solution)/shard_map/reduce_scatter | solution.py:49
  23.9 45.5 %copy-start.38 = (f32[128]{0:T(128)}, f32[128]{0:T(128)S(1)}, u32[]{:S(2)}) copy-start(f32[128]{0:T(128)S(1)} %get-tuple-element.45) | copy-start | bytes 1540
  23.9 45.5 %copy-start.40 = (f32[128]{0:T(128)}, f32[128]{0:T(128)S(1)}, u32[]{:S(2)}) copy-start(f32[128]{0:T(128)S(1)} %get-tuple-element.46) | copy-start | bytes 1540
  23.9 47.4 %copy-start.36 = (f32[128]{0:T(128)}, f32[128]{0:T(128)S(1)}, u32[]{:S(2)}) copy-start(f32[128]{0:T(128)S(1)} %get-tuple-element.44) | copy-start | bytes 1540
  69.3 183.3 %all-reduce.13.cloned.1.call-start = ((), (), s32[]{:S(2)}) async-start(), calls=%async_computation.14 | async-start | bytes 14155776
  101.4 195.6 %all-gather.14.cloned.1.call-start = ((), (), s32[]{:S(2)}) async-start(), calls=%async_computation.10 | async-start | bytes 2949120 | tf_op jit(solution)/shard_map/all_gather | solution.py:45
  259.3 67.5 %all-gather.12.cloned.1.call-start = ((), (), s32[]{:S(2)}) async-start(), calls=%async_computation.8 | async-start | bytes 1474560 | tf_op jit(solution)/shard_map/all_gather | solution.py:45
  259.9 77.3 %reduce-scatter.13.cloned.1.call-start = ((), (), s32[]{:S(2)}) async-start(), calls=%async_computation.11 | async-start | bytes 393216 | tf_op jit(solution)/shard_map/reduce_scatter | solution.py:49
  317.4 32.3 %reduce-scatter.11.cloned.1.call-start = ((), (), s32[]{:S(2)}) async-start(), calls=%async_computation.9 | async-start | bytes 393216 | tf_op jit(solution)/shard_map/reduce_scatter | solution.py:49
  329.3 28.2 %copy-start.5 = (bf16[256,1,2304]{0,2,1:T(8,128)(2,1)S(1)}, bf16[256,1,2304]{0,2,1:T(8,128)(2,1)}, u32[]{:S(2)}) copy-start(bf16[256,1,2304]{0,2,1:T(8,128)(2,1)} %all-gather.12.cloned.1.call-done) | copy-start | bytes 3538948
  329.4 52.5 %reduce-scatter.15.cloned.1.call-start = ((), (), s32[]{:S(2)}) async-start(), calls=%async_computation.12 | async-start | bytes 655360 | tf_op jit(solution)/shard_map/reduce_scatter | solution.py:41
  356.2 55.1 %reduce-scatter.17.cloned.1.call-start = ((), (), s32[]{:S(2)}) async-start(), calls=%async_computation.13 | async-start | bytes 393216 | tf_op jit(solution)/shard_map/reduce_scatter | solution.py:49
  362.3 19.6 %copy-start.12 = (f32[256,128]{1,0:T(8,128)S(1)}, f32[256,128]{1,0:T(8,128)}, u32[]{:S(2)}) copy-start(f32[256,128]{1,0:T(8,128)} %copy-done.11) | copy-start | bytes 393220
  362.3 19.6 %copy-start.27 = (f32[256,128]{1,0:T(8,128)S(1)}, f32[256,128]{1,0:T(8,128)}, u32[]{:S(2)}) copy-start(f32[256,128]{1,0:T(8,128)} %get-tuple-element.34) | copy-start | bytes 393220
  362.3 20.6 %copy-start.44 = (f32[254]{0:T(256)S(1)}, f32[254]{0:T(256)}, u32[]{:S(2)}) copy-start(f32[254]{0:T(256)} %slice.89) | copy-start | bytes 3052
  362.3 20.7 %copy-start.43 = (f32[255]{0:T(256)S(1)}, f32[255]{0:T(256)}, u32[]{:S(2)}) copy-start(f32[255]{0:T(256)} %slice.87) | copy-start | bytes 3064
  395.9 329.7 %all-reduce.15.cloned.1.call-start = ((), (), s32[]{:S(2)}) async-start(), calls=%async_computation.15 | async-start | bytes 18350080 | tf_op jit(solution)/shard_map/psum | solution.py:184
  398.9 20.3 %copy-start.42 = (f32[256]{0:T(256)S(1)}, f32[256]{0:T(256)}, u32[]{:S(2)}) copy-start(f32[256]{0:T(256)} %get-tuple-element.10) | copy-start | bytes 3076
  398.9 35.4 %copy-start.28 = (f32[128,256]{1,0:T(8,128)S(1)}, f32[128,256]{1,0:T(8,128)}, u32[]{:S(2)}) copy-start(f32[128,256]{1,0:T(8,128)} %get-tuple-element.30) | copy-start | bytes 393220
  398.9 35.4 %copy-start.46 = (f32[128]{0:T(128)S(1)}, f32[128]{0:T(128)}, u32[]{:S(2)}) copy-start(f32[128]{0:T(128)} %get-tuple-element.47) | copy-start | bytes 1540
  (34 other events, 219.8 us)
Sparse Core Ops, SparseCore 0:
  23.7 31.4 reduce-scatter.6
  69.4 7.7 reduce-scatter.8
  101.5 151.0 all-reduce.12
  259.4 37.4 all-gather.13
  299.2 27.5 all-gather.11
  329.5 7.7 reduce-scatter.12
  340.1 8.8 reduce-scatter.10
  356.3 25.4 reduce-scatter.14
  396.0 7.7 reduce-scatter.16
  407.9 317.6 all-reduce.14
